TPU v7x, 256 devices: a whole 4x4x8 slice. The times are simulated.
256 devices in a mesh: acq: 128 (over x, z, y), slab: 2 (over core).
Axes of the slice: x: 4, y: 4, z: 8, core: 2. Of those that a mesh axis runs over, the one named last changes fastest.
Arguments:
- slc_amplitude: float32 [256, 160, 1280], P('acq', None, 'slab'), may hold values from 0.3 to 3
- slc_phase: float32 [256, 160, 1280], P('acq', None, 'slab'), may hold values from -9.5 to 9.5
- pair_list: int32 [512, 2], replicated, may hold values from 0 to 255, as said below
- pair_owner: int32 [512], replicated, may hold values from 0 to 127, as said below
- tile_map: int32 [128], replicated, may hold values from 0 to 127, as said below
Outputs:
- interferograms: float32 [512, 2, 32, 256], P('acq', None, None, 'slab')
- linked_phases: float32 [256, 2, 32, 256], P('acq', None, None, 'slab')
- tile_quality: float32 [256, 2, 32], P('acq', 'slab')
Inputs may be any that keep to these rules, and one draw needn't show every extreme that they name: `pair_list`: each row is (r, s) with r < s. One of the two acquisitions is held by the pair's owner and the other by the owner or by a device beside it along acq; every device but the first owns a pair whose other acquisition is held by the device before it, and every device but the last owns one whose other acquisition is held by the device after it. `pair_owner`: every device owns exactly 4 pairs. `tile_map`: every device owns at most 2 tiles, and some device owns exactly 2.
All inputs are finite; a program needn't handle non-finite values.
Results may differ from a plain program's by a relative error of at most 0.0001.
Values sent between devices are 32-bit elements; how exact they have to be, the bound alone decides.
A program may use at most 64 MiB of HBM per device.

v0:
```python
from functools import partial

import jax
import jax.numpy as jnp
from jax import lax
from jax.experimental import pallas as pl
from jax.experimental.pallas import tpu as pltpu
from jax.sharding import PartitionSpec as P

MESH = pl.DeviceIdType.MESH
F32 = jnp.float32
BF16 = jnp.bfloat16
LOOK = 5
ITERS = 8
TILE_CAP = 2
EPS = 1e-06
HALO = 8
LANES = 128
SUB = 8
GROUP = SUB * LOOK


def sincos(x):
    turns = jnp.floor(x * 0.6366197723675814 + 0.5)
    r = ((x - turns * 1.5703125) - turns * 4.837512969970703e-4) - turns * 7.54978995489188e-8
    z = r * r
    s = ((-1.9515295891e-4 * z + 8.3321608736e-3) * z - 1.6666654611e-1) * z * r + r
    c = ((2.443315711809948e-5 * z - 1.388731625493765e-3) * z + 4.166664568298827e-2) * z * z
    c = c - 0.5 * z + 1.0
    quarter = turns.astype(jnp.int32)
    odd = (quarter & 1) == 1
    sin = jnp.where(odd, c, s)
    cos = jnp.where(odd, s, c)
    sin = jnp.where((quarter & 2) == 2, -sin, sin)
    cos = jnp.where(((quarter + 1) & 2) == 2, -cos, cos)
    return sin, cos


def total(x):
    return jnp.sum(jnp.sum(x, axis=1, keepdims=True), axis=0, keepdims=True)


def smallest(x):
    return jnp.min(jnp.min(x, axis=1, keepdims=True), axis=0, keepdims=True)


def kernel(
    tab_ref, amp_hbm, ph_hbm, ifg_ref, link_ref, qual_ref,
    amp, ph, smp, from_left, from_right, acc, win, gee, power, loc, emsg, ebuf, lmsg, lbuf,
    edge, vec, deg, umsg, ubuf, nmsg, nbuf, amsg, abuf,
    in_sem, s_send, s_recv, g_send, g_recv, e_send, h_send, e_recv, l_send, lh_send, l_recv,
    u_send, u_recv, n_send, n_recv, a_send, a_recv,
):
    devices = lax.axis_size("acq")
    columns = loc.shape[1]
    planes = devices // columns
    half = columns // 2
    rows_w = columns + 2 * HALO
    lane_tiles = smp.shape[2]
    pairs_total = 4 * devices
    acq_total = 2 * devices
    me = lax.axis_index("acq")
    plane = me // columns
    cs = lax.rem(me, columns)
    right = lax.rem(me + 1, devices)
    left = lax.rem(me + devices - 1, devices)
    above = lax.rem(plane + 1, planes)
    below = lax.rem(plane + planes - 1, planes)

    def remote(src, dst, send, recv, target):
        return pltpu.make_async_remote_copy(
            src_ref=src, dst_ref=dst, send_sem=send, recv_sem=recv,
            device_id={"acq": target}, device_id_type=MESH,
        )

    def await_bytes(ref, sem):
        pltpu.make_async_copy(ref, ref, sem).wait()

    order = (0, 2, 1, 3)
    for g in order:
        for a, (src, dst) in enumerate(((amp_hbm, amp), (ph_hbm, ph))):
            cut = pl.ds(g * GROUP, GROUP)
            pltpu.make_async_copy(src.at[:, cut, :], dst.at[:, cut, :], in_sem.at[a, g]).start()

    barrier = pltpu.get_barrier_semaphore()

    def tell(target):
        pl.semaphore_signal(barrier, inc=1, device_id={"acq": target}, device_id_type=MESH)

    tell(left)
    tell(right)

    @pl.loop(1, columns)
    def _(i):
        tell(plane * columns + lax.rem(cs + i, columns))

    for i in range(1, planes):
        tell(lax.rem(plane + i, planes) * columns + cs)

    @pl.loop(0, HALO + 1)
    def _(i):
        tell(above * columns + i)

    @pl.loop(0, HALO)
    def _(i):
        tell(below * columns + columns - HALO + i)

    def form_samples(g):
        for a, (src, dst) in enumerate(((amp_hbm, amp), (ph_hbm, ph))):
            cut = pl.ds(g * GROUP, GROUP)
            pltpu.make_async_copy(src.at[:, cut, :], dst.at[:, cut, :], in_sem.at[a, g]).wait()

        @pl.loop(0, LOOK)
        def _(i):
            cut = pl.ds(pl.multiple_of(g * GROUP + i * SUB, SUB), SUB)
            here = pl.ds(pl.multiple_of(i * SUB, SUB), SUB)
            for a in range(2):
                size = amp[a, cut, :]
                sin, cos = sincos(ph[a, cut, :])
                real, imag = size * cos, size * sin
                for lt in range(lane_tiles):
                    lanes = slice(lt * LANES, (lt + 1) * LANES)
                    smp[g, 2 * a, lt, here, :] = real[:, lanes]
                    smp[g, 2 * a + 1, lt, here, :] = imag[:, lanes]

    def sample_copy(side, k):
        if side == 0:
            return remote(smp.at[k], from_left.at[k], s_send.at[0, k], s_recv.at[0, k], right)
        return remote(smp.at[2 + k], from_right.at[k], s_send.at[1, k], s_recv.at[1, k], left)

    form_samples(0)
    form_samples(2)
    in_halo = jnp.logical_or(cs <= HALO, cs >= columns - HALO).astype(jnp.int32)
    pl.semaphore_wait(barrier, 2 + (columns - 1) + (planes - 1) + columns * in_halo)
    sample_copy(0, 0).start()
    sample_copy(1, 0).start()
    form_samples(1)
    form_samples(3)
    sample_copy(0, 1).start()
    sample_copy(1, 1).start()

    raw = lax.broadcasted_iota(jnp.int32, win.shape, 0)
    low = lax.broadcasted_iota(jnp.int32, win.shape, 1) * LOOK
    win[...] = jnp.where((raw >= low) & (raw < low + LOOK), 1.0, 0.0).astype(BF16)

    def look(count):
        x = acc[0:count, :]
        high = x.astype(BF16)
        rest = (x - high.astype(F32)).astype(BF16)
        return jnp.dot(high, win[...], preferred_element_type=F32) + jnp.dot(
            rest, win[...], preferred_element_type=F32
        )

    key = tab_ref[0:4, :] * 256 + tab_ref[4:8, :]
    base = 2 * me

    def key_of(i, j):
        return (base + i) * 256 + base + j

    codes = [[key_of(i - 2, j) for i in range(2) for j in range(2)],
             [key_of(i, j + 2) for i in range(2) for j in range(2)]]
    code_own = key_of(0, 1)

    def count_of(code):
        return total(jnp.where(key == code, 1.0, 0.0))

    weight = [[count_of(c) for c in side] for side in codes]
    weight_own = count_of(code_own)

    index = (
        lax.broadcasted_iota(jnp.int32, (4, LANES), 0) * LANES
        + lax.broadcasted_iota(jnp.int32, (4, LANES), 1)
    ).astype(F32)
    key_f = key.astype(F32)
    big = 1e6
    left_over = jnp.where(tab_ref[8:12, :] == me, index, big)
    slot_key = []
    for _ in range(4):
        first = smallest(left_over)
        hit = index == first
        slot_key.append(total(jnp.where(hit, key_f, 0.0)).astype(jnp.int32))
        left_over = jnp.where(hit, big, left_over)

    ones = jnp.ones((LANES, LANES), BF16)
    window_dev = lax.rem(
        lax.broadcasted_iota(jnp.int32, (rows_w, LANES), 0)
        + (plane * columns + devices - HALO),
        devices,
    )
    for i in range(2):
        acq = 2 * window_dev + i
        hits = jnp.zeros((rows_w, LANES), F32)
        for q in range(8):
            hits = hits + jnp.where(acq == tab_ref[q : q + 1, :], 1.0, 0.0)
        deg[i] = 1.0 + jnp.dot(hits.astype(BF16), ones, preferred_element_type=F32)

    @pl.loop(0, 4)
    def _(g):
        @pl.loop(0, lane_tiles)
        def _(lt):
            lanes = pl.ds(pl.multiple_of(lt * LANES, LANES), LANES)
            sums = [jnp.zeros((SUB, LANES), F32) for _ in range(4)]
            for kk in range(LOOK):
                x = [smp[g, f, lt, pl.ds(kk, SUB, stride=LOOK), :] for f in range(4)]
                sums[0] = sums[0] + (x[0] * x[0] + x[1] * x[1])
                sums[1] = sums[1] + (x[2] * x[2] + x[3] * x[3])
                sums[2] = sums[2] + (x[0] * x[2] + x[1] * x[3])
                sums[3] = sums[3] + (x[1] * x[2] - x[0] * x[3])
            for f in range(4):
                acc[f * SUB : (f + 1) * SUB, lanes] = sums[f]

        out = look(4 * SUB)
        cut = pl.ds(pl.multiple_of(g * SUB, SUB), SUB)
        power_ref, power_sec = out[0:SUB], out[SUB : 2 * SUB]
        power[0, cut, :] = power_ref
        power[1, cut, :] = power_sec
        scale = 1.0 / jnp.sqrt(power_ref * power_sec)
        loc[0, cut, :] = out[2 * SUB : 3 * SUB] * scale
        loc[1, cut, :] = out[3 * SUB : 4 * SUB] * scale

    for f in range(2):
        lmsg[:, f, :] = loc[f] * weight_own

    here = HALO + cs

    @pl.loop(1, columns)
    def _(i):
        c = lax.rem(cs + i, columns)
        remote(lmsg.at[c], lbuf.at[here], l_send, l_recv, plane * columns + c).start()

    @pl.when(cs < HALO)
    def _():
        @pl.loop(0, columns)
        def _(i):
            c = lax.rem(cs + i, columns)
            remote(
                lmsg.at[c], lbuf.at[columns + HALO + cs], lh_send, l_recv, below * columns + c
            ).start()

    @pl.when(cs >= columns - HALO)
    def _():
        @pl.loop(0, columns)
        def _(i):
            c = lax.rem(cs + i, columns)
            remote(
                lmsg.at[c], lbuf.at[cs - (columns - HALO)], lh_send, l_recv, above * columns + c
            ).start()

    lbuf[here] = lmsg[cs]

    vec[...] = jnp.zeros_like(vec)
    vec[0, 0] = jnp.ones(vec.shape[2:], F32)
    vec[0, 2] = jnp.ones(vec.shape[2:], F32)
    for f in range(8):
        edge[f, 0:SUB, :] = jnp.zeros((SUB, LANES), F32)

    def gee_copy(side, k):
        if side == 0:
            part = gee.at[0, :, pl.ds(SUB * k, SUB), :]
            return remote(
                part, gee.at[1, :, pl.ds(SUB * k, SUB), :], g_send.at[0, k], g_recv.at[0, k], left
            )
        part = gee.at[1, :, pl.ds(half + SUB * k, SUB), :]
        return remote(
            part, gee.at[0, :, pl.ds(half + SUB * k, SUB), :],
            g_send.at[1, k], g_recv.at[1, k], right,
        )

    def slot_rows(slot):
        return pl.ds(pl.multiple_of(SUB * slot, SUB), SUB)

    for k in range(2):
        for side in range(2):
            sample_copy(side, k).wait_recv()
            other = (from_left, from_right)[side]
            first_col = side * half + k * SUB

            @pl.loop(0, lane_tiles)
            def _(lt):
                lanes = pl.ds(pl.multiple_of(lt * LANES, LANES), LANES)
                sums = [jnp.zeros((SUB, LANES), F32) for _ in range(10)]
                for kk in range(LOOK):
                    cut = pl.ds(kk, SUB, stride=LOOK)
                    near = [smp[2 * side + k, f, lt, cut, :] for f in range(4)]
                    far = [other[k, f, lt, cut, :] for f in range(4)]
                    ref, sec = (far, near) if side == 0 else (near, far)
                    for i in range(2):
                        for j in range(2):
                            f = (2 * i + j) * 2
                            sums[f] = sums[f] + (
                                ref[2 * i] * sec[2 * j] + ref[2 * i + 1] * sec[2 * j + 1]
                            )
                            sums[f + 1] = sums[f + 1] + (
                                ref[2 * i + 1] * sec[2 * j] - ref[2 * i] * sec[2 * j + 1]
                            )
                        sums[8 + i] = sums[8 + i] + (
                            far[2 * i] * far[2 * i] + far[2 * i + 1] * far[2 * i + 1]
                        )
                for f in range(10):
                    acc[f * SUB : (f + 1) * SUB, lanes] = sums[f]

            out = look(10 * SUB)
            for i in range(2):
                for j in range(2):
                    mine, theirs = (j, i) if side == 0 else (i, j)
                    scale = 1.0 / jnp.sqrt(
                        power[mine, first_col : first_col + SUB, :]
                        * out[(8 + theirs) * SUB : (9 + theirs) * SUB]
                    )
                    for part in range(2):
                        f = (2 * i + j) * 2 + part
                        value = out[f * SUB : (f + 1) * SUB] * scale
                        gee[side, f, first_col : first_col + SUB, :] = value
                        emsg[pl.ds(SUB * first_col + f, SUB, stride=SUB), :] = (
                            value * weight[side][2 * i + j]
                        )

            edge_at = cs - 1 if side == 0 else cs

            @pl.loop(0, SUB)
            def _(i):
                c = first_col + lax.rem(cs + i, SUB)
                src = emsg.at[slot_rows(c), :]

                @pl.when(c != cs)
                def _():
                    remote(
                        src, ebuf.at[slot_rows(HALO + edge_at), :], e_send, e_recv,
                        plane * columns + c,
                    ).start()

                @pl.when(edge_at < HALO)
                def _():
                    remote(
                        src, ebuf.at[slot_rows(columns + HALO + edge_at), :], h_send, e_recv,
                        below * columns + c,
                    ).start()

                @pl.when(edge_at >= columns - HALO)
                def _():
                    remote(
                        src, ebuf.at[slot_rows(edge_at - (columns - HALO)), :], h_send, e_recv,
                        above * columns + c,
                    ).start()

        for side in range(2):
            gee_copy(side, k).start()

    shift = (cs < half).astype(jnp.int32)
    ebuf[slot_rows(here - shift), :] = emsg[slot_rows(cs), :]

    await_bytes(lbuf.at[pl.ds(0, rows_w - 1)], l_recv)
    await_bytes(ebuf.at[pl.ds(0, (rows_w - 1) * SUB), :], e_recv)
    for f in range(8):
        for t in range(rows_w // SUB):
            edge[f, SUB * (t + 1) : SUB * (t + 2), :] = ebuf[
                pl.ds(f + SUB * SUB * t, SUB, stride=SUB), :
            ]
    loc_w = [lbuf[:, f, :] for f in range(2)]
    for f in range(2):
        edge[8 + f, SUB : SUB + rows_w, :] = loc_w[f]

    def step(t, kappa):
        now = lax.rem(t, 2)
        size = jnp.zeros((SUB, LANES), F32)
        for w in range(rows_w // SUB):
            cut = slice(SUB * w, SUB * (w + 1))
            mid = slice(SUB * (w + 1), SUB * (w + 2))
            low = slice(SUB * (w + 1) - 1, SUB * (w + 2) - 1)
            high = slice(SUB * (w + 1) + 1, SUB * (w + 2) + 1)
            u = [vec[now, f, mid, :] for f in range(4)]
            u_low = [vec[now, f, low, :] for f in range(4)]
            u_high = [vec[now, f, high, :] for f in range(4)]
            lr, li = edge[8, mid, :], edge[9, mid, :]
            for a in range(2):
                d = deg[a, cut, :]
                o = 1 - a
                sign = 1.0 if a == 0 else -1.0
                re = d * u[2 * a] + lr * u[2 * o] - sign * (li * u[2 * o + 1])
                im = d * u[2 * a + 1] + lr * u[2 * o + 1] + sign * (li * u[2 * o])
                for b in range(2):
                    f = (2 * a + b) * 2
                    gr, gi = edge[f, mid, :], edge[f + 1, mid, :]
                    re = re + (gr * u_high[2 * b] - gi * u_high[2 * b + 1])
                    im = im + (gr * u_high[2 * b + 1] + gi * u_high[2 * b])
                    f = (2 * b + a) * 2
                    gr, gi = edge[f, low, :], edge[f + 1, low, :]
                    re = re + (gr * u_low[2 * b] + gi * u_low[2 * b + 1])
                    im = im + (gr * u_low[2 * b + 1] - gi * u_low[2 * b])
                vec[1 - now, 2 * a, mid, :] = re
                vec[1 - now, 2 * a + 1, mid, :] = im
                if HALO // SUB <= w < (HALO + columns) // SUB:
                    size = size + (re * re + im * im)
        return (jnp.sum(size, axis=0, keepdims=True) + EPS * kappa) / acq_total

    kappa = lax.fori_loop(0, ITERS, step, jnp.full((1, LANES), 1.0 / planes, F32))
    last = ITERS % 2
    nmsg[0:1, :] = kappa

    own = slice(SUB + HALO, SUB + HALO + columns)
    for f in range(4):
        umsg[:, f, :] = vec[last, f, own, :]

    @pl.loop(1, columns)
    def _(i):
        c = lax.rem(cs + i, columns)
        remote(umsg.at[c], ubuf.at[cs], u_send, u_recv, plane * columns + c).start()

    qual = jnp.zeros((SUB, LANES), F32)
    for w in range(HALO // SUB, (HALO + columns) // SUB):
        mid = slice(SUB * (w + 1), SUB * (w + 2))
        high = slice(SUB * (w + 1) + 1, SUB * (w + 2) + 1)
        u = [vec[last, f, mid, :] for f in range(4)]
        u_high = [vec[last, f, high, :] for f in range(4)]
        qual = qual + edge[8, mid, :] * (u[0] * u[2] + u[1] * u[3])
        qual = qual - edge[9, mid, :] * (u[0] * u[3] - u[1] * u[2])
        for a in range(2):
            for b in range(2):
                f = (2 * a + b) * 2
                ur, ui = u[2 * a], u[2 * a + 1]
                vr, vi = u_high[2 * b], u_high[2 * b + 1]
                qual = qual + edge[f, mid, :] * (ur * vr + ui * vi)
                qual = qual - edge[f + 1, mid, :] * (ur * vi - ui * vr)
    nmsg[1:2, :] = jnp.sum(qual, axis=0, keepdims=True)
    for i in range(1, planes):
        target = lax.rem(plane + i, planes) * columns + cs
        remote(nmsg, nbuf.at[plane], n_send, n_recv, target).start()
    nbuf[plane] = nmsg[...]
    ubuf[cs] = umsg[cs]

    for side in range(2):
        for k in range(2):
            gee_copy(side, k).wait_recv()
    for slot in range(4):
        hit_own = slot_key[slot] == code_own
        hits = [[slot_key[slot] == c for c in side] for side in codes]

        @pl.loop(0, columns // SUB)
        def _(g):
            cut = pl.ds(pl.multiple_of(g * SUB, SUB), SUB)
            for part in range(2):
                value = jnp.where(hit_own, loc[part, cut, :], 0.0)
                for side in range(2):
                    for c in range(4):
                        value = jnp.where(hits[side][c], gee[side, 2 * c + part, cut, :], value)
                ifg_ref[slot, part, cut, :] = value

    await_bytes(nbuf.at[pl.ds(0, planes - 1)], n_recv)
    both = nbuf[0]
    for i in range(1, planes):
        both = both + nbuf[i]
    kappa, qual = both[0:1, :], both[1:2, :]
    amsg[0:1, :] = 1.0 / jnp.sqrt(kappa)
    amsg[1:2, :] = qual / (kappa * pairs_total)

    @pl.loop(1, columns)
    def _(i):
        c = lax.rem(cs + i, columns)
        remote(amsg, abuf.at[cs], a_send, a_recv, plane * columns + c).start()

    abuf[cs] = amsg[...]

    tile = lax.broadcasted_iota(jnp.int32, (1, LANES), 1).astype(F32)
    free = jnp.where(tab_ref[12:13, :] == me, tile, big)
    picks = []
    for _ in range(TILE_CAP):
        first = jnp.min(free, axis=1, keepdims=True)
        hit = tile == first
        picks.append(jnp.where(hit, 1.0, 0.0))
        free = jnp.where(hit, big, free)

    await_bytes(ubuf.at[pl.ds(0, columns - 1)], u_recv)
    await_bytes(abuf.at[pl.ds(0, columns - 1)], a_recv)
    alpha = abuf[:, 0, :]
    for a in range(2):
        for part in range(2):
            link_ref[a, part] = ubuf[:, 2 * a + part, :] * alpha
    quality = abuf[:, 1, :]
    pick = jnp.concatenate(picks + [jnp.zeros((SUB - TILE_CAP, LANES), F32)], axis=0)
    chosen = lax.dot_general(
        pick, quality, (((1,), (1,)), ((), ())),
        precision=lax.Precision.HIGHEST, preferred_element_type=F32,
    )
    for a in range(TILE_CAP):
        qual_ref[a] = chosen[a : a + 1, :]

    for side in range(2):
        for k in range(2):
            sample_copy(side, k).wait_send()
            gee_copy(side, k).wait_send()
    await_bytes(lmsg.at[pl.ds(0, columns - 1)], l_send)
    await_bytes(emsg.at[pl.ds(0, (columns - 1) * SUB), :], e_send)
    await_bytes(ubuf.at[pl.ds(0, columns - 1)], u_send)
    await_bytes(abuf.at[pl.ds(0, columns - 1)], a_send)
    await_bytes(nbuf.at[pl.ds(0, planes - 1)], n_send)

    @pl.when(jnp.logical_or(cs < HALO, cs >= columns - HALO))
    def _():
        await_bytes(lmsg, lh_send)

    for side in range(2):
        edge_at = cs - 1 if side == 0 else cs

        @pl.when(jnp.logical_or(edge_at < HALO, edge_at >= columns - HALO))
        def _():
            await_bytes(emsg.at[pl.ds(0, half * SUB), :], h_send)


def per_device(slc_amplitude, slc_phase, pair_list, pair_owner, tile_map):
    columns = slc_amplitude.shape[1] // LOOK
    raw = slc_amplitude.shape[2]
    table = jnp.concatenate([pair_list.T.reshape(-1), pair_owner, tile_map]).reshape(-1, LANES)
    rows_w = columns + 2 * HALO
    dma = pltpu.SemaphoreType.DMA
    vmem = pl.BlockSpec(memory_space=pltpu.VMEM)
    return tuple(
        pl.pallas_call(
            kernel,
            name="phase_linking",
            out_shape=(
                jax.ShapeDtypeStruct((4, 2, columns, LANES), F32),
                jax.ShapeDtypeStruct((2, 2, columns, LANES), F32),
                jax.ShapeDtypeStruct((TILE_CAP, 1, columns), F32),
            ),
            in_specs=[vmem, pl.BlockSpec(memory_space=pl.ANY), pl.BlockSpec(memory_space=pl.ANY)],
            out_specs=(vmem, vmem, vmem),
            scratch_shapes=[
                pltpu.VMEM(slc_amplitude.shape, F32),
                pltpu.VMEM(slc_amplitude.shape, F32),
                pltpu.VMEM((4, 4, raw // LANES, GROUP, LANES), F32),
                pltpu.VMEM((2, 4, raw // LANES, GROUP, LANES), F32),
                pltpu.VMEM((2, 4, raw // LANES, GROUP, LANES), F32),
                pltpu.VMEM((10 * SUB, raw), F32),
                pltpu.VMEM((raw, LANES), BF16),
                pltpu.VMEM((2, 8, columns, LANES), F32),
                pltpu.VMEM((2, columns, LANES), F32),
                pltpu.VMEM((2, columns, LANES), F32),
                pltpu.VMEM((columns * SUB, LANES), F32),
                pltpu.VMEM((rows_w * SUB, LANES), F32),
                pltpu.VMEM((columns, 2, LANES), F32),
                pltpu.VMEM((rows_w, 2, LANES), F32),
                pltpu.VMEM((10, rows_w + 2 * SUB, LANES), F32),
                pltpu.VMEM((2, 4, rows_w + 2 * SUB, LANES), F32),
                pltpu.VMEM((2, rows_w, LANES), F32),
                pltpu.VMEM((columns, 4, LANES), F32),
                pltpu.VMEM((columns, 4, LANES), F32),
                pltpu.VMEM((2, LANES), F32),
                pltpu.VMEM((4, 2, LANES), F32),
                pltpu.VMEM((2, LANES), F32),
                pltpu.VMEM((columns, 2, LANES), F32),
                dma((2, 4)), dma((2, 2)), dma((2, 2)), dma((2, 2)), dma((2, 2)),
                dma, dma, dma, dma, dma, dma, dma, dma, dma, dma, dma, dma,
            ],
            compiler_params=pltpu.CompilerParams(
                collective_id=0, has_side_effects=True, vmem_limit_bytes=40 * 2**20
            ),
        )(table, slc_amplitude, slc_phase)
    )


def solution(mesh):
    in_specs = (P("acq", None, "slab"), P("acq", None, "slab"), P(), P(), P())
    out_specs = (P("acq", None, None, "slab"), P("acq", None, None, "slab"), P("acq", "slab", None))
    return jax.shard_map(
        per_device, mesh=mesh, in_specs=in_specs, out_specs=out_specs, check_vma=False
    )
```

profile of v0, /device:TPU:32, one launch (start us, length us, event | category | flops | bytes accessed | tf_op | source)
XLA Modules:
  0.0 62.9 jit_solution(14868978347013524058)
XLA Ops:
  0.6 0.0 copy-start.2
  0.6 0.7 %copy.8 = s32[1,4,2,128]{3,1,2,0:T(4,128)S(1)} copy(s32[1,4,2,128]{3,2,1,0:T(2,128)} %bitcast.6) | data formatting | bytes 8192
  1.3 0.0 copy-start.3
  1.3 0.0 copy-done.2
  1.3 0.7 %copy-done.3 = s32[128]{0:T(128)S(1)} copy-done((s32[128]{0:T(128)S(1)}, s32[128]{0:T(128)}, u32[]{:S(2)}) %copy-start.3) | copy-done | bytes 536
  2.0 0.0 copy-start
  2.0 1.1 %copy-done = f32[2,160,640]{2,1,0:T(8,128)S(1)} copy-done((f32[2,160,640]{2,1,0:T(8,128)S(1)}, f32[2,160,640]{2,1,0:T(8,128)}, u32[]{:S(2)}) %copy-start) | copy-done | bytes 819224
  3.1 0.0 copy-start.1
  3.1 1.1 %copy-done.1 = f32[2,160,640]{2,1,0:T(8,128)S(1)} copy-done((f32[2,160,640]{2,1,0:T(8,128)S(1)}, f32[2,160,640]{2,1,0:T(8,128)}, u32[]{:S(2)}) %copy-start.1) | copy-done | bytes 819224
  4.3 56.8 %phase_linking.1 = (f32[4,2,32,128]{3,2,1,0:T(8,128)S(1)}, f32[2,2,32,128]{3,2,1,0:T(8,128)S(1)}, f32[2,1,32]{2,1,0:T(1,128)S(1)}) custom-call(s32[13,128]{1,0:T(8,128)S(1)} %add_bitcast_fusion.tab_ref, f32[2,160,640]{2,1,0:T(8,128)S(1)} %copy-done, f32[2,160,640]{2,1,0:T(8,128)S(1)} %copy-done.1), custom_call_target="tpu_custom_call" | custom-call | tf_op jit(solution)/shard_map/phase_linking/pallas_call | solution.py:517
  61.0 0.7 %copy.12 = f32[4,2,32,128]{3,2,1,0:T(8,128)} copy(f32[4,2,32,128]{3,2,1,0:T(8,128)S(1)} %get-tuple-element.6) | data formatting | bytes 262144
  61.7 0.6 copy.13
  62.3 0.6 copy.14
  (1 shorter events, 0.0 us)
Async XLA Ops:
  0.6 0.7 %copy-start.2 = (s32[512]{0:T(512)S(1)}, s32[512]{0:T(512)}, u32[]{:S(2)}) copy-start(s32[512]{0:T(512)} %param.8) | copy-start | bytes 6148
  1.3 0.7 %copy-start.3 = (s32[128]{0:T(128)S(1)}, s32[128]{0:T(128)}, u32[]{:S(2)}) copy-start(s32[128]{0:T(128)} %param.9) | copy-start | bytes 1540
  2.0 1.1 %copy-start = (f32[2,160,640]{2,1,0:T(8,128)S(1)}, f32[2,160,640]{2,1,0:T(8,128)}, u32[]{:S(2)}) copy-start(f32[2,160,640]{2,1,0:T(8,128)} %amp_hbm.1) | copy-start | bytes 2457604
  3.1 1.1 %copy-start.1 = (f32[2,160,640]{2,1,0:T(8,128)S(1)}, f32[2,160,640]{2,1,0:T(8,128)}, u32[]{:S(2)}) copy-start(f32[2,160,640]{2,1,0:T(8,128)} %ph_hbm.1) | copy-start | bytes 2457604
where the time goes:
time: 63.1 us; the launch traced here: 62.9 us
  Pallas kernels  56.8 us (90%)
  local copies, waits for them, and re-layouts  5.49 us (9%)
  between operations  0.65 us (1%)
    pallas_call x1, Pallas kernels, per_device(): pl.pallas_call(kernel, name='phase_linking', out_shape=(jax.ShapeDtypeStr...  56.8 us
    unnamed x12, local copies, waits for them, and re-layouts  5.49 us

commit v1 on v0

--- a/solution.py
+++ b/solution.py
@@ -45,10 +45,10 @@
 
 
 def kernel(
-    tab_ref, amp_hbm, ph_hbm, ifg_ref, link_ref, qual_ref,
-    amp, ph, smp, from_left, from_right, acc, win, gee, power, loc, emsg, ebuf, lmsg, lbuf,
+    amp_hbm, ph_hbm, pair_hbm, owner_hbm, tile_hbm, ifg_ref, link_ref, qual_ref,
+    amp, ph, pair_tab, owner_tab, tile_tab, smp, from_left, from_right, acc, win, gee, power, loc, emsg, ebuf, lmsg, lbuf,
     edge, vec, deg, umsg, ubuf, nmsg, nbuf, amsg, abuf,
-    in_sem, s_send, s_recv, g_send, g_recv, e_send, h_send, e_recv, l_send, lh_send, l_recv,
+    in_sem, tab_sem, s_send, s_recv, g_send, g_recv, e_send, h_send, e_recv, l_send, lh_send, l_recv,
     u_send, u_recv, n_send, n_recv, a_send, a_recv,
 ):
     devices = lax.axis_size("acq")
@@ -82,6 +82,10 @@
             cut = pl.ds(g * GROUP, GROUP)
             pltpu.make_async_copy(src.at[:, cut, :], dst.at[:, cut, :], in_sem.at[a, g]).start()
 
+    tables = ((pair_hbm, pair_tab), (owner_hbm, owner_tab), (tile_hbm, tile_tab))
+    for i, (src, dst) in enumerate(tables):
+        pltpu.make_async_copy(src, dst, tab_sem.at[i]).start()
+
     barrier = pltpu.get_barrier_semaphore()
 
     def tell(target):
@@ -151,7 +155,10 @@
             rest, win[...], preferred_element_type=F32
         )
 
-    key = tab_ref[0:4, :] * 256 + tab_ref[4:8, :]
+    for i, (src, dst) in enumerate(tables):
+        pltpu.make_async_copy(src, dst, tab_sem.at[i]).wait()
+    pair_ref, pair_sec = pair_tab[:, 0, :], pair_tab[:, 1, :]
+    key = pair_ref * 256 + pair_sec
     base = 2 * me
 
     def key_of(i, j):
@@ -173,7 +180,7 @@
     ).astype(F32)
     key_f = key.astype(F32)
     big = 1e6
-    left_over = jnp.where(tab_ref[8:12, :] == me, index, big)
+    left_over = jnp.where(owner_tab[...] == me, index, big)
     slot_key = []
     for _ in range(4):
         first = smallest(left_over)
@@ -190,8 +197,9 @@
     for i in range(2):
         acq = 2 * window_dev + i
         hits = jnp.zeros((rows_w, LANES), F32)
-        for q in range(8):
-            hits = hits + jnp.where(acq == tab_ref[q : q + 1, :], 1.0, 0.0)
+        for member in (pair_ref, pair_sec):
+            for q in range(4):
+                hits = hits + jnp.where(acq == member[q : q + 1, :], 1.0, 0.0)
         deg[i] = 1.0 + jnp.dot(hits.astype(BF16), ones, preferred_element_type=F32)
 
     @pl.loop(0, 4)
@@ -397,15 +405,6 @@
     last = ITERS % 2
     nmsg[0:1, :] = kappa
 
-    own = slice(SUB + HALO, SUB + HALO + columns)
-    for f in range(4):
-        umsg[:, f, :] = vec[last, f, own, :]
-
-    @pl.loop(1, columns)
-    def _(i):
-        c = lax.rem(cs + i, columns)
-        remote(umsg.at[c], ubuf.at[cs], u_send, u_recv, plane * columns + c).start()
-
     qual = jnp.zeros((SUB, LANES), F32)
     for w in range(HALO // SUB, (HALO + columns) // SUB):
         mid = slice(SUB * (w + 1), SUB * (w + 2))
@@ -425,6 +424,15 @@
     for i in range(1, planes):
         target = lax.rem(plane + i, planes) * columns + cs
         remote(nmsg, nbuf.at[plane], n_send, n_recv, target).start()
+    own = slice(SUB + HALO, SUB + HALO + columns)
+    for f in range(4):
+        umsg[:, f, :] = vec[last, f, own, :]
+
+    @pl.loop(1, columns)
+    def _(i):
+        c = lax.rem(cs + i, columns)
+        remote(umsg.at[c], ubuf.at[cs], u_send, u_recv, plane * columns + c).start()
+
     nbuf[plane] = nmsg[...]
     ubuf[cs] = umsg[cs]
 
@@ -461,7 +469,7 @@
     abuf[cs] = amsg[...]
 
     tile = lax.broadcasted_iota(jnp.int32, (1, LANES), 1).astype(F32)
-    free = jnp.where(tab_ref[12:13, :] == me, tile, big)
+    free = jnp.where(tile_tab[...] == me, tile, big)
     picks = []
     for _ in range(TILE_CAP):
         first = jnp.min(free, axis=1, keepdims=True)
@@ -506,56 +514,83 @@
             await_bytes(emsg.at[pl.ds(0, half * SUB), :], h_send)
 
 
+def write_out(ifg_in, link_in, qual_in, ifg_out, link_out, qual_out, sem):
+    copies = [
+        pltpu.make_async_copy(src, dst, sem.at[i])
+        for i, (src, dst) in enumerate(
+            ((ifg_in, ifg_out), (link_in, link_out), (qual_in, qual_out))
+        )
+    ]
+    for copy in copies:
+        copy.start()
+    for copy in copies:
+        copy.wait()
+
+
 def per_device(slc_amplitude, slc_phase, pair_list, pair_owner, tile_map):
     columns = slc_amplitude.shape[1] // LOOK
     raw = slc_amplitude.shape[2]
-    table = jnp.concatenate([pair_list.T.reshape(-1), pair_owner, tile_map]).reshape(-1, LANES)
+    pairs = pair_list.reshape(-1, LANES, 2).transpose(0, 2, 1)
+    owners = pair_owner.reshape(-1, LANES)
+    tiles = tile_map.reshape(-1, LANES)
+    hbm = pl.BlockSpec(memory_space=pltpu.HBM)
     rows_w = columns + 2 * HALO
     dma = pltpu.SemaphoreType.DMA
     vmem = pl.BlockSpec(memory_space=pltpu.VMEM)
-    return tuple(
-        pl.pallas_call(
-            kernel,
-            name="phase_linking",
-            out_shape=(
-                jax.ShapeDtypeStruct((4, 2, columns, LANES), F32),
-                jax.ShapeDtypeStruct((2, 2, columns, LANES), F32),
-                jax.ShapeDtypeStruct((TILE_CAP, 1, columns), F32),
-            ),
-            in_specs=[vmem, pl.BlockSpec(memory_space=pl.ANY), pl.BlockSpec(memory_space=pl.ANY)],
-            out_specs=(vmem, vmem, vmem),
-            scratch_shapes=[
-                pltpu.VMEM(slc_amplitude.shape, F32),
-                pltpu.VMEM(slc_amplitude.shape, F32),
-                pltpu.VMEM((4, 4, raw // LANES, GROUP, LANES), F32),
-                pltpu.VMEM((2, 4, raw // LANES, GROUP, LANES), F32),
-                pltpu.VMEM((2, 4, raw // LANES, GROUP, LANES), F32),
-                pltpu.VMEM((10 * SUB, raw), F32),
-                pltpu.VMEM((raw, LANES), BF16),
-                pltpu.VMEM((2, 8, columns, LANES), F32),
-                pltpu.VMEM((2, columns, LANES), F32),
-                pltpu.VMEM((2, columns, LANES), F32),
-                pltpu.VMEM((columns * SUB, LANES), F32),
-                pltpu.VMEM((rows_w * SUB, LANES), F32),
-                pltpu.VMEM((columns, 2, LANES), F32),
-                pltpu.VMEM((rows_w, 2, LANES), F32),
-                pltpu.VMEM((10, rows_w + 2 * SUB, LANES), F32),
-                pltpu.VMEM((2, 4, rows_w + 2 * SUB, LANES), F32),
-                pltpu.VMEM((2, rows_w, LANES), F32),
-                pltpu.VMEM((columns, 4, LANES), F32),
-                pltpu.VMEM((columns, 4, LANES), F32),
-                pltpu.VMEM((2, LANES), F32),
-                pltpu.VMEM((4, 2, LANES), F32),
-                pltpu.VMEM((2, LANES), F32),
-                pltpu.VMEM((columns, 2, LANES), F32),
-                dma((2, 4)), dma((2, 2)), dma((2, 2)), dma((2, 2)), dma((2, 2)),
-                dma, dma, dma, dma, dma, dma, dma, dma, dma, dma, dma, dma,
-            ],
-            compiler_params=pltpu.CompilerParams(
-                collective_id=0, has_side_effects=True, vmem_limit_bytes=40 * 2**20
-            ),
-        )(table, slc_amplitude, slc_phase)
-    )
+    arguments = (slc_amplitude, slc_phase, pairs, owners, tiles)
+    results = pl.pallas_call(
+        kernel,
+        name="phase_linking",
+        out_shape=(
+            jax.ShapeDtypeStruct((4, 2, columns, LANES), F32),
+            jax.ShapeDtypeStruct((2, 2, columns, LANES), F32),
+            jax.ShapeDtypeStruct((TILE_CAP, 1, columns), F32),
+        ),
+        in_specs=[hbm] * 5,
+        out_specs=(vmem, vmem, vmem),
+        scratch_shapes=[
+            pltpu.VMEM(slc_amplitude.shape, F32),
+            pltpu.VMEM(slc_amplitude.shape, F32),
+            pltpu.VMEM(pairs.shape, jnp.int32),
+            pltpu.VMEM(owners.shape, jnp.int32),
+            pltpu.VMEM(tiles.shape, jnp.int32),
+            pltpu.VMEM((4, 4, raw // LANES, GROUP, LANES), F32),
+            pltpu.VMEM((2, 4, raw // LANES, GROUP, LANES), F32),
+            pltpu.VMEM((2, 4, raw // LANES, GROUP, LANES), F32),
+            pltpu.VMEM((10 * SUB, raw), F32),
+            pltpu.VMEM((raw, LANES), BF16),
+            pltpu.VMEM((2, 8, columns, LANES), F32),
+            pltpu.VMEM((2, columns, LANES), F32),
+            pltpu.VMEM((2, columns, LANES), F32),
+            pltpu.VMEM((columns * SUB, LANES), F32),
+            pltpu.VMEM((rows_w * SUB, LANES), F32),
+            pltpu.VMEM((columns, 2, LANES), F32),
+            pltpu.VMEM((rows_w, 2, LANES), F32),
+            pltpu.VMEM((10, rows_w + 2 * SUB, LANES), F32),
+            pltpu.VMEM((2, 4, rows_w + 2 * SUB, LANES), F32),
+            pltpu.VMEM((2, rows_w, LANES), F32),
+            pltpu.VMEM((columns, 4, LANES), F32),
+            pltpu.VMEM((columns, 4, LANES), F32),
+            pltpu.VMEM((2, LANES), F32),
+            pltpu.VMEM((4, 2, LANES), F32),
+            pltpu.VMEM((2, LANES), F32),
+            pltpu.VMEM((columns, 2, LANES), F32),
+            dma((2, 4)), dma((3,)), dma((2, 2)), dma((2, 2)), dma((2, 2)), dma((2, 2)),
+            dma, dma, dma, dma, dma, dma, dma, dma, dma, dma, dma, dma,
+        ],
+        compiler_params=pltpu.CompilerParams(
+            collective_id=0, has_side_effects=True, vmem_limit_bytes=40 * 2**20
+        ),
+    )(*[pltpu.with_memory_space_constraint(x, pltpu.HBM) for x in arguments])
+    return pl.pallas_call(
+        write_out,
+        name="write_out",
+        out_shape=[jax.ShapeDtypeStruct(x.shape, F32) for x in results],
+        in_specs=[vmem] * 3,
+        out_specs=[hbm] * 3,
+        scratch_shapes=[dma((3,))],
+        compiler_params=pltpu.CompilerParams(vmem_limit_bytes=2**20),
+    )(*results)
 
 
 def solution(mesh):

time: 63.1 us -> 56.8 us (0.900)
  local copies, waits for them, and re-layouts: 5.49 us -> 0 us
  Pallas kernels: 56.8 us -> 56.1 us
    unnamed x12 -> x0, local copies, waits for them, and re-layouts: 5.49 us -> none
    pallas_call x1, Pallas kernels: 56.8 us -> 55.4 us  [per_device(): pl.pallas_call(kernel, name='phase_linking', out_shape=(jax.ShapeDtypeStr...]
    pallas_call x0 -> x1, Pallas kernels: none -> 0.7 us  [per_device(): pl.pallas_call(write_out, name='write_out', out_shape=[jax.ShapeDtypeStru...]
where the time goes in v1:
time: 56.8 us; the launch traced here: 56.7 us
  Pallas kernels  56.1 us (99%)
  between operations  0.64 us (1%)
    pallas_call x1, Pallas kernels, per_device(): pl.pallas_call(kernel, name='phase_linking', out_shape=(jax.ShapeDtypeStr...  55.4 us

profile of v1, /device:TPU:32, one launch (start us, length us, event | category | flops | bytes accessed | tf_op | source)
XLA Modules:
  0.0 56.7 jit_solution(4184595011595954967)
XLA Ops:
  0.6 55.4 %phase_linking.1 = (f32[4,2,32,128]{3,2,1,0:T(8,128)S(1)}, f32[2,2,32,128]{3,2,1,0:T(8,128)S(1)}, f32[2,1,32]{2,1,0:T(1,128)S(1)}) custom-call(f32[2,160,640]{2,1,0:T(8,128)} %amp_hbm.1, f32[2,160,640]{2,1,0:T(8,128)} %ph_hbm.1, s32[4,2,128]{2,1,0:T(2,128)} %bitcast.5, s32[4,128]{1,0:T(4,128)} %bitcast.6, s32[1,128]{1,0:T(1,128)} %bitcast.7), custom_call_target="tpu_custom_call" | custom-call | tf_op jit(solution)/shard_map/phase_linking/pallas_call | solution.py:541
  56.0 0.7 %write_out.1 = (f32[4,2,32,128]{3,2,1,0:T(8,128)}, f32[2,2,32,128]{3,2,1,0:T(8,128)}, f32[2,1,32]{2,1,0:T(1,128)}) custom-call(f32[4,2,32,128]{3,2,1,0:T(8,128)S(1)} %get-tuple-element.6.ifg_in, f32[2,2,32,128]{3,2,1,0:T(8,128)S(1)} %get-tuple-element.7.link_in, f32[2,1,32]{2,1,0:T(1,128)S(1)} %get-tuple-element.8.qual_in), custom_call_target="tpu_custom_call" | custom-call | tf_op jit(solution)/shard_map/write_out/pallas_call | solution.py:585

commit v2 on v1

--- a/solution.py
+++ b/solution.py
@@ -14,6 +14,9 @@
 ITERS = 8
 TILE_CAP = 2
 EPS = 1e-06
+BACK = 6
+SLOT = 16
+ROWS = 10
 HALO = 8
 LANES = 128
 SUB = 8
@@ -46,10 +49,10 @@
 
 def kernel(
     amp_hbm, ph_hbm, pair_hbm, owner_hbm, tile_hbm, ifg_ref, link_ref, qual_ref,
-    amp, ph, pair_tab, owner_tab, tile_tab, smp, from_left, from_right, acc, win, gee, power, loc, emsg, ebuf, lmsg, lbuf,
-    edge, vec, deg, umsg, ubuf, nmsg, nbuf, amsg, abuf,
-    in_sem, tab_sem, s_send, s_recv, g_send, g_recv, e_send, h_send, e_recv, l_send, lh_send, l_recv,
-    u_send, u_recv, n_send, n_recv, a_send, a_recv,
+    amp, ph, pair_tab, owner_tab, tile_tab, smp, from_left, from_right, acc, win, gee, power, loc, emsg, ebuf,
+    edge, vec, deg, umsg, ubuf, nmsg, nbuf, pick, chosen,
+    in_sem, tab_sem, s_send, s_recv, g_send, g_recv, ready,
+    e_send, h_send, e_recv, u_send, u_recv, n_send, n_recv,
 ):
     devices = lax.axis_size("acq")
     columns = loc.shape[1]
@@ -94,20 +97,15 @@
     tell(left)
     tell(right)
 
-    @pl.loop(1, columns)
-    def _(i):
-        tell(plane * columns + lax.rem(cs + i, columns))
-
-    for i in range(1, planes):
-        tell(lax.rem(plane + i, planes) * columns + cs)
-
-    @pl.loop(0, HALO + 1)
-    def _(i):
-        tell(above * columns + i)
-
-    @pl.loop(0, HALO)
-    def _(i):
-        tell(below * columns + columns - HALO + i)
+    def say(r):
+        for target in (me + 2**r, me + devices - 2**r):
+            pl.semaphore_signal(
+                ready.at[r], inc=1, device_id={"acq": lax.rem(target, devices)},
+                device_id_type=MESH,
+            )
+
+    def hear(r):
+        pl.semaphore_wait(ready.at[r], 2)
 
     def form_samples(g):
         for a, (src, dst) in enumerate(((amp_hbm, amp), (ph_hbm, ph))):
@@ -134,14 +132,17 @@
 
     form_samples(0)
     form_samples(2)
-    in_halo = jnp.logical_or(cs <= HALO, cs >= columns - HALO).astype(jnp.int32)
-    pl.semaphore_wait(barrier, 2 + (columns - 1) + (planes - 1) + columns * in_halo)
+    pl.semaphore_wait(barrier, 2)
     sample_copy(0, 0).start()
     sample_copy(1, 0).start()
+    say(0)
     form_samples(1)
     form_samples(3)
     sample_copy(0, 1).start()
     sample_copy(1, 1).start()
+
+    hear(0)
+    say(1)
 
     raw = lax.broadcasted_iota(jnp.int32, win.shape, 0)
     low = lax.broadcasted_iota(jnp.int32, win.shape, 1) * LOOK
@@ -154,6 +155,9 @@
         return jnp.dot(high, win[...], preferred_element_type=F32) + jnp.dot(
             rest, win[...], preferred_element_type=F32
         )
+
+    hear(1)
+    say(2)
 
     for i, (src, dst) in enumerate(tables):
         pltpu.make_async_copy(src, dst, tab_sem.at[i]).wait()
@@ -188,6 +192,9 @@
         slot_key.append(total(jnp.where(hit, key_f, 0.0)).astype(jnp.int32))
         left_over = jnp.where(hit, big, left_over)
 
+    hear(2)
+    say(3)
+
     ones = jnp.ones((LANES, LANES), BF16)
     window_dev = lax.rem(
         lax.broadcasted_iota(jnp.int32, (rows_w, LANES), 0)
@@ -201,6 +208,18 @@
             for q in range(4):
                 hits = hits + jnp.where(acq == member[q : q + 1, :], 1.0, 0.0)
         deg[i] = 1.0 + jnp.dot(hits.astype(BF16), ones, preferred_element_type=F32)
+
+    tile = lax.broadcasted_iota(jnp.int32, (SUB, LANES), 1).astype(F32)
+    place = lax.broadcasted_iota(jnp.int32, (SUB, LANES), 0)
+    holder = (place // TILE_CAP) * columns + cs
+    free = jnp.where(tile_tab[...] == holder, tile, big)
+    first = jnp.min(free, axis=1, keepdims=True)
+    second = jnp.min(jnp.where(tile == first, big, free), axis=1, keepdims=True)
+    wanted = jnp.where(lax.rem(place, TILE_CAP) == 0, first, second)
+    pick[...] = jnp.where(tile == wanted, 1.0, 0.0)
+
+    hear(3)
+    say(4)
 
     @pl.loop(0, 4)
     def _(g):
@@ -227,40 +246,20 @@
         loc[1, cut, :] = out[3 * SUB : 4 * SUB] * scale
 
     for f in range(2):
-        lmsg[:, f, :] = loc[f] * weight_own
-
-    here = HALO + cs
-
-    @pl.loop(1, columns)
-    def _(i):
-        c = lax.rem(cs + i, columns)
-        remote(lmsg.at[c], lbuf.at[here], l_send, l_recv, plane * columns + c).start()
-
-    @pl.when(cs < HALO)
-    def _():
-        @pl.loop(0, columns)
-        def _(i):
-            c = lax.rem(cs + i, columns)
-            remote(
-                lmsg.at[c], lbuf.at[columns + HALO + cs], lh_send, l_recv, below * columns + c
-            ).start()
-
-    @pl.when(cs >= columns - HALO)
-    def _():
-        @pl.loop(0, columns)
-        def _(i):
-            c = lax.rem(cs + i, columns)
-            remote(
-                lmsg.at[c], lbuf.at[cs - (columns - HALO)], lh_send, l_recv, above * columns + c
-            ).start()
-
-    lbuf[here] = lmsg[cs]
+        for g in range(columns // SUB):
+            emsg[pl.ds(SLOT * SUB * g + 8 + f, SUB, stride=SLOT), :] = (
+                loc[f, SUB * g : SUB * (g + 1), :] * weight_own
+            )
+
+    hear(4)
+    say(5)
 
     vec[...] = jnp.zeros_like(vec)
     vec[0, 0] = jnp.ones(vec.shape[2:], F32)
     vec[0, 2] = jnp.ones(vec.shape[2:], F32)
     for f in range(8):
         edge[f, 0:SUB, :] = jnp.zeros((SUB, LANES), F32)
+    ebuf[0:SLOT, :] = jnp.zeros((SLOT, LANES), F32)
 
     def gee_copy(side, k):
         if side == 0:
@@ -275,7 +274,12 @@
         )
 
     def slot_rows(slot):
-        return pl.ds(pl.multiple_of(SUB * slot, SUB), SUB)
+        return pl.ds(pl.multiple_of(SLOT * slot, SLOT), ROWS)
+
+    def window_rows(slot):
+        return slot_rows(slot + 1)
+
+    hear(5)
 
     for k in range(2):
         for side in range(2):
@@ -319,7 +323,7 @@
                         f = (2 * i + j) * 2 + part
                         value = out[f * SUB : (f + 1) * SUB] * scale
                         gee[side, f, first_col : first_col + SUB, :] = value
-                        emsg[pl.ds(SUB * first_col + f, SUB, stride=SUB), :] = (
+                        emsg[pl.ds(SLOT * first_col + f, SUB, stride=SLOT), :] = (
                             value * weight[side][2 * i + j]
                         )
 
@@ -333,21 +337,21 @@
                 @pl.when(c != cs)
                 def _():
                     remote(
-                        src, ebuf.at[slot_rows(HALO + edge_at), :], e_send, e_recv,
+                        src, ebuf.at[window_rows(HALO + edge_at), :], e_send, e_recv,
                         plane * columns + c,
                     ).start()
 
                 @pl.when(edge_at < HALO)
                 def _():
                     remote(
-                        src, ebuf.at[slot_rows(columns + HALO + edge_at), :], h_send, e_recv,
+                        src, ebuf.at[window_rows(columns + HALO + edge_at), :], h_send, e_recv,
                         below * columns + c,
                     ).start()
 
                 @pl.when(edge_at >= columns - HALO)
                 def _():
                     remote(
-                        src, ebuf.at[slot_rows(edge_at - (columns - HALO)), :], h_send, e_recv,
+                        src, ebuf.at[window_rows(edge_at - (columns - HALO)), :], h_send, e_recv,
                         above * columns + c,
                     ).start()
 
@@ -355,18 +359,15 @@
             gee_copy(side, k).start()
 
     shift = (cs < half).astype(jnp.int32)
-    ebuf[slot_rows(here - shift), :] = emsg[slot_rows(cs), :]
-
-    await_bytes(lbuf.at[pl.ds(0, rows_w - 1)], l_recv)
-    await_bytes(ebuf.at[pl.ds(0, (rows_w - 1) * SUB), :], e_recv)
-    for f in range(8):
+    ebuf[window_rows(HALO + cs - shift), :] = emsg[slot_rows(cs), :]
+
+    await_bytes(ebuf.at[pl.ds(0, (rows_w - 1) * ROWS), :], e_recv)
+    for f in range(ROWS):
+        back_by = shift if f >= 8 else 0
         for t in range(rows_w // SUB):
             edge[f, SUB * (t + 1) : SUB * (t + 2), :] = ebuf[
-                pl.ds(f + SUB * SUB * t, SUB, stride=SUB), :
+                pl.ds(f + SLOT * (SUB * t + 1 - back_by), SUB, stride=SLOT), :
             ]
-    loc_w = [lbuf[:, f, :] for f in range(2)]
-    for f in range(2):
-        edge[8 + f, SUB : SUB + rows_w, :] = loc_w[f]
 
     def step(t, kappa):
         now = lax.rem(t, 2)
@@ -403,8 +404,6 @@
 
     kappa = lax.fori_loop(0, ITERS, step, jnp.full((1, LANES), 1.0 / planes, F32))
     last = ITERS % 2
-    nmsg[0:1, :] = kappa
-
     qual = jnp.zeros((SUB, LANES), F32)
     for w in range(HALO // SUB, (HALO + columns) // SUB):
         mid = slice(SUB * (w + 1), SUB * (w + 2))
@@ -420,21 +419,27 @@
                 vr, vi = u_high[2 * b], u_high[2 * b + 1]
                 qual = qual + edge[f, mid, :] * (ur * vr + ui * vi)
                 qual = qual - edge[f + 1, mid, :] * (ur * vi - ui * vr)
-    nmsg[1:2, :] = jnp.sum(qual, axis=0, keepdims=True)
-    for i in range(1, planes):
-        target = lax.rem(plane + i, planes) * columns + cs
-        remote(nmsg, nbuf.at[plane], n_send, n_recv, target).start()
-    own = slice(SUB + HALO, SUB + HALO + columns)
-    for f in range(4):
-        umsg[:, f, :] = vec[last, f, own, :]
+    qual = jnp.sum(qual, axis=0, keepdims=True)
+
+    for g in range(columns // SUB):
+        cut = slice(SUB + HALO + SUB * g, SUB + HALO + SUB * (g + 1))
+        for f in range(4):
+            umsg[pl.ds(SUB * SUB * g + f, SUB, stride=SUB), :] = vec[last, f, cut, :]
+        umsg[pl.ds(SUB * SUB * g + 4, SUB, stride=SUB), :] = jnp.broadcast_to(kappa, (SUB, LANES))
+        umsg[pl.ds(SUB * SUB * g + 5, SUB, stride=SUB), :] = jnp.broadcast_to(qual, (SUB, LANES))
+
+    def back_rows(slot):
+        return pl.ds(pl.multiple_of(SUB * slot, SUB), BACK)
 
     @pl.loop(1, columns)
     def _(i):
         c = lax.rem(cs + i, columns)
-        remote(umsg.at[c], ubuf.at[cs], u_send, u_recv, plane * columns + c).start()
-
-    nbuf[plane] = nmsg[...]
-    ubuf[cs] = umsg[cs]
+        remote(
+            umsg.at[back_rows(c), :], ubuf.at[back_rows(cs), :], u_send, u_recv,
+            plane * columns + c,
+        ).start()
+
+    ubuf[back_rows(cs), :] = umsg[back_rows(cs), :]
 
     for side in range(2):
         for k in range(2):
@@ -453,65 +458,58 @@
                         value = jnp.where(hits[side][c], gee[side, 2 * c + part, cut, :], value)
                 ifg_ref[slot, part, cut, :] = value
 
+    def back(f, g):
+        return ubuf[pl.ds(SUB * SUB * g + f, SUB, stride=SUB), :]
+
+    def picked(x):
+        return lax.dot_general(
+            pick[...], x, (((1,), (1,)), ((), ())),
+            precision=lax.Precision.HIGHEST, preferred_element_type=F32,
+        )
+
+    await_bytes(ubuf.at[pl.ds(0, (columns - 1) * BACK), :], u_recv)
+    for g in range(columns // SUB):
+        nmsg[SUB * g : SUB * (g + 1), :] = back(4, g)
+    quality = jnp.concatenate([back(5, g) for g in range(columns // SUB)], axis=0)
+    nmsg[columns : columns + SUB, 0:columns] = picked(quality)
+    nmsg[columns : columns + SUB, columns:] = jnp.zeros((SUB, LANES - columns), F32)
+    for i in range(1, planes):
+        target = lax.rem(plane + i, planes) * columns + cs
+        remote(nmsg, nbuf.at[plane], n_send, n_recv, target).start()
+    nbuf[plane] = nmsg[...]
+
     await_bytes(nbuf.at[pl.ds(0, planes - 1)], n_recv)
-    both = nbuf[0]
+    scale = nbuf[0]
     for i in range(1, planes):
-        both = both + nbuf[i]
-    kappa, qual = both[0:1, :], both[1:2, :]
-    amsg[0:1, :] = 1.0 / jnp.sqrt(kappa)
-    amsg[1:2, :] = qual / (kappa * pairs_total)
-
-    @pl.loop(1, columns)
-    def _(i):
-        c = lax.rem(cs + i, columns)
-        remote(amsg, abuf.at[cs], a_send, a_recv, plane * columns + c).start()
-
-    abuf[cs] = amsg[...]
-
-    tile = lax.broadcasted_iota(jnp.int32, (1, LANES), 1).astype(F32)
-    free = jnp.where(tile_tab[...] == me, tile, big)
-    picks = []
-    for _ in range(TILE_CAP):
-        first = jnp.min(free, axis=1, keepdims=True)
-        hit = tile == first
-        picks.append(jnp.where(hit, 1.0, 0.0))
-        free = jnp.where(hit, big, free)
-
-    await_bytes(ubuf.at[pl.ds(0, columns - 1)], u_recv)
-    await_bytes(abuf.at[pl.ds(0, columns - 1)], a_recv)
-    alpha = abuf[:, 0, :]
-    for a in range(2):
-        for part in range(2):
-            link_ref[a, part] = ubuf[:, 2 * a + part, :] * alpha
-    quality = abuf[:, 1, :]
-    pick = jnp.concatenate(picks + [jnp.zeros((SUB - TILE_CAP, LANES), F32)], axis=0)
-    chosen = lax.dot_general(
-        pick, quality, (((1,), (1,)), ((), ())),
-        precision=lax.Precision.HIGHEST, preferred_element_type=F32,
+        scale = scale + nbuf[i]
+    kappa = scale[0:columns]
+    alpha = 1.0 / jnp.sqrt(kappa)
+    for g in range(columns // SUB):
+        cut = slice(SUB * g, SUB * (g + 1))
+        for f in range(4):
+            link_ref[f // 2, f % 2, cut, :] = back(f, g) * alpha[cut]
+    norm = picked(kappa) * pairs_total
+    held = norm > 0.0
+    chosen[...] = jnp.where(
+        held, scale[columns:, 0:columns] / jnp.where(held, norm, 1.0), 0.0
     )
     for a in range(TILE_CAP):
-        qual_ref[a] = chosen[a : a + 1, :]
+        qual_ref[a] = chosen[pl.ds(plane * TILE_CAP + a, 1), :]
 
     for side in range(2):
         for k in range(2):
             sample_copy(side, k).wait_send()
             gee_copy(side, k).wait_send()
-    await_bytes(lmsg.at[pl.ds(0, columns - 1)], l_send)
-    await_bytes(emsg.at[pl.ds(0, (columns - 1) * SUB), :], e_send)
-    await_bytes(ubuf.at[pl.ds(0, columns - 1)], u_send)
-    await_bytes(abuf.at[pl.ds(0, columns - 1)], a_send)
+    await_bytes(emsg.at[pl.ds(0, (columns - 1) * ROWS), :], e_send)
+    await_bytes(ubuf.at[pl.ds(0, (columns - 1) * BACK), :], u_send)
     await_bytes(nbuf.at[pl.ds(0, planes - 1)], n_send)
-
-    @pl.when(jnp.logical_or(cs < HALO, cs >= columns - HALO))
-    def _():
-        await_bytes(lmsg, lh_send)
 
     for side in range(2):
         edge_at = cs - 1 if side == 0 else cs
 
         @pl.when(jnp.logical_or(edge_at < HALO, edge_at >= columns - HALO))
         def _():
-            await_bytes(emsg.at[pl.ds(0, half * SUB), :], h_send)
+            await_bytes(emsg.at[pl.ds(0, half * ROWS), :], h_send)
 
 
 def write_out(ifg_in, link_in, qual_in, ifg_out, link_out, qual_out, sem):
@@ -535,6 +533,7 @@
     tiles = tile_map.reshape(-1, LANES)
     hbm = pl.BlockSpec(memory_space=pltpu.HBM)
     rows_w = columns + 2 * HALO
+    planes = lax.axis_size("acq") // columns
     dma = pltpu.SemaphoreType.DMA
     vmem = pl.BlockSpec(memory_space=pltpu.VMEM)
     arguments = (slc_amplitude, slc_phase, pairs, owners, tiles)
@@ -562,21 +561,19 @@
             pltpu.VMEM((2, 8, columns, LANES), F32),
             pltpu.VMEM((2, columns, LANES), F32),
             pltpu.VMEM((2, columns, LANES), F32),
-            pltpu.VMEM((columns * SUB, LANES), F32),
-            pltpu.VMEM((rows_w * SUB, LANES), F32),
-            pltpu.VMEM((columns, 2, LANES), F32),
-            pltpu.VMEM((rows_w, 2, LANES), F32),
+            pltpu.VMEM((columns * SLOT, LANES), F32),
+            pltpu.VMEM(((rows_w + 1) * SLOT, LANES), F32),
             pltpu.VMEM((10, rows_w + 2 * SUB, LANES), F32),
             pltpu.VMEM((2, 4, rows_w + 2 * SUB, LANES), F32),
             pltpu.VMEM((2, rows_w, LANES), F32),
-            pltpu.VMEM((columns, 4, LANES), F32),
-            pltpu.VMEM((columns, 4, LANES), F32),
-            pltpu.VMEM((2, LANES), F32),
-            pltpu.VMEM((4, 2, LANES), F32),
-            pltpu.VMEM((2, LANES), F32),
-            pltpu.VMEM((columns, 2, LANES), F32),
+            pltpu.VMEM((columns * SUB, LANES), F32),
+            pltpu.VMEM((columns * SUB, LANES), F32),
+            pltpu.VMEM((columns + SUB, LANES), F32),
+            pltpu.VMEM((planes, columns + SUB, LANES), F32),
+            pltpu.VMEM((SUB, LANES), F32),
+            pltpu.VMEM((SUB, columns), F32),
             dma((2, 4)), dma((3,)), dma((2, 2)), dma((2, 2)), dma((2, 2)), dma((2, 2)),
-            dma, dma, dma, dma, dma, dma, dma, dma, dma, dma, dma, dma,
+            pltpu.SemaphoreType.REGULAR((6,)), dma, dma, dma, dma, dma, dma, dma,
         ],
         compiler_params=pltpu.CompilerParams(
             collective_id=0, has_side_effects=True, vmem_limit_bytes=40 * 2**20

time: 56.8 us -> 53.8 us (0.947)
  Pallas kernels: 56.1 us -> 53.1 us
    pallas_call x1, Pallas kernels: 55.4 us -> 52.4 us  [per_device(): pl.pallas_call(kernel, name='phase_linking', out_shape=(jax.ShapeDtypeStr...]
where the time goes in v2:
time: 53.8 us; the launch traced here: 53.7 us
  Pallas kernels  53.1 us (99%)
  between operations  0.64 us (1%)
    pallas_call x1, Pallas kernels, per_device(): pl.pallas_call(kernel, name='phase_linking', out_shape=(jax.ShapeDtypeStr...  52.4 us

profile of v2, /device:TPU:32, one launch (start us, length us, event | category | flops | bytes accessed | tf_op | source)
XLA Modules:
  0.0 53.7 jit_solution(6903237884118143223)
XLA Ops:
  0.6 52.4 %phase_linking.1 = (f32[4,2,32,128]{3,2,1,0:T(8,128)S(1)}, f32[2,2,32,128]{3,2,1,0:T(8,128)S(1)}, f32[2,1,32]{2,1,0:T(1,128)S(1)}) custom-call(f32[2,160,640]{2,1,0:T(8,128)} %amp_hbm.1, f32[2,160,640]{2,1,0:T(8,128)} %ph_hbm.1, s32[4,2,128]{2,1,0:T(2,128)} %bitcast.5, s32[4,128]{1,0:T(4,128)} %bitcast.6, s32[1,128]{1,0:T(1,128)} %bitcast.7), custom_call_target="tpu_custom_call" | custom-call | tf_op jit(solution)/shard_map/phase_linking/pallas_call | solution.py:540
  53.0 0.7 %write_out.1 = (f32[4,2,32,128]{3,2,1,0:T(8,128)}, f32[2,2,32,128]{3,2,1,0:T(8,128)}, f32[2,1,32]{2,1,0:T(1,128)}) custom-call(f32[4,2,32,128]{3,2,1,0:T(8,128)S(1)} %get-tuple-element.6.ifg_in, f32[2,2,32,128]{3,2,1,0:T(8,128)S(1)} %get-tuple-element.7.link_in, f32[2,1,32]{2,1,0:T(1,128)S(1)} %get-tuple-element.8.qual_in), custom_call_target="tpu_custom_call" | custom-call | tf_op jit(solution)/shard_map/write_out/pallas_call | solution.py:582

commit v3 on v2

--- a/solution.py
+++ b/solution.py
@@ -63,12 +63,18 @@
     pairs_total = 4 * devices
     acq_total = 2 * devices
     me = lax.axis_index("acq")
-    plane = me // columns
-    cs = lax.rem(me, columns)
-    right = lax.rem(me + 1, devices)
-    left = lax.rem(me + devices - 1, devices)
-    above = lax.rem(plane + 1, planes)
-    below = lax.rem(plane + planes - 1, planes)
+    assert columns & (columns - 1) == 0 and planes & (planes - 1) == 0
+
+    def wrap(x, size):
+        return x & (size - 1)
+
+    plane = me >> (columns.bit_length() - 1)
+    cs = wrap(me, columns)
+    first_of_plane = me - cs
+    right = wrap(me + 1, devices)
+    left = wrap(me + devices - 1, devices)
+    above = wrap(first_of_plane + columns, devices)
+    below = wrap(first_of_plane + devices - columns, devices)
 
     def remote(src, dst, send, recv, target):
         return pltpu.make_async_remote_copy(
@@ -100,7 +106,7 @@
     def say(r):
         for target in (me + 2**r, me + devices - 2**r):
             pl.semaphore_signal(
-                ready.at[r], inc=1, device_id={"acq": lax.rem(target, devices)},
+                ready.at[r], inc=1, device_id={"acq": wrap(target, devices)},
                 device_id_type=MESH,
             )
 
@@ -133,13 +139,26 @@
     form_samples(0)
     form_samples(2)
     pl.semaphore_wait(barrier, 2)
-    sample_copy(0, 0).start()
-    sample_copy(1, 0).start()
+    core = lax.axis_index("slab")
     say(0)
+
+    @pl.when(core == 0)
+    def _():
+        sample_copy(0, 0).start()
+        sample_copy(1, 0).start()
+
     form_samples(1)
     form_samples(3)
-    sample_copy(0, 1).start()
-    sample_copy(1, 1).start()
+
+    @pl.when(core == 0)
+    def _():
+        sample_copy(0, 1).start()
+        sample_copy(1, 1).start()
+
+    @pl.when(core == 1)
+    def _():
+        sample_copy(0, 0).start()
+        sample_copy(1, 0).start()
 
     hear(0)
     say(1)
@@ -220,6 +239,11 @@
 
     hear(3)
     say(4)
+
+    @pl.when(core == 1)
+    def _():
+        sample_copy(0, 1).start()
+        sample_copy(1, 1).start()
 
     @pl.loop(0, 4)
     def _(g):
@@ -280,6 +304,7 @@
         return slot_rows(slot + 1)
 
     hear(5)
+
 
     for k in range(2):
         for side in range(2):
@@ -331,28 +356,28 @@
 
             @pl.loop(0, SUB)
             def _(i):
-                c = first_col + lax.rem(cs + i, SUB)
+                c = first_col + wrap(cs + i, SUB)
                 src = emsg.at[slot_rows(c), :]
+
+                @pl.when(edge_at < HALO)
+                def _():
+                    remote(
+                        src, ebuf.at[window_rows(columns + HALO + edge_at), :], h_send, e_recv,
+                        below + c,
+                    ).start()
+
+                @pl.when(edge_at >= columns - HALO)
+                def _():
+                    remote(
+                        src, ebuf.at[window_rows(edge_at - (columns - HALO)), :], h_send, e_recv,
+                        above + c,
+                    ).start()
 
                 @pl.when(c != cs)
                 def _():
                     remote(
                         src, ebuf.at[window_rows(HALO + edge_at), :], e_send, e_recv,
-                        plane * columns + c,
-                    ).start()
-
-                @pl.when(edge_at < HALO)
-                def _():
-                    remote(
-                        src, ebuf.at[window_rows(columns + HALO + edge_at), :], h_send, e_recv,
-                        below * columns + c,
-                    ).start()
-
-                @pl.when(edge_at >= columns - HALO)
-                def _():
-                    remote(
-                        src, ebuf.at[window_rows(edge_at - (columns - HALO)), :], h_send, e_recv,
-                        above * columns + c,
+                        first_of_plane + c,
                     ).start()
 
         for side in range(2):
@@ -433,10 +458,10 @@
 
     @pl.loop(1, columns)
     def _(i):
-        c = lax.rem(cs + i, columns)
+        c = wrap(cs + i, columns)
         remote(
             umsg.at[back_rows(c), :], ubuf.at[back_rows(cs), :], u_send, u_recv,
-            plane * columns + c,
+            first_of_plane + c,
         ).start()
 
     ubuf[back_rows(cs), :] = umsg[back_rows(cs), :]

time: 53.8 us -> 52.9 us (0.983)
  Pallas kernels: 53.1 us -> 51.9 us
    pallas_call x1, Pallas kernels: 52.4 us -> 51.2 us  [per_device(): pl.pallas_call(kernel, name='phase_linking', out_shape=(jax.ShapeDtypeStr...]
where the time goes in v3:
time: 52.9 us; the launch traced here: 52.6 us
  Pallas kernels  51.9 us (98%)
  between operations  0.64 us (1%)
    pallas_call x1, Pallas kernels, per_device(): pl.pallas_call(kernel, name='phase_linking', out_shape=(jax.ShapeDtypeStr...  51.2 us

profile of v3, /device:TPU:32, one launch (start us, length us, event | category | flops | bytes accessed | tf_op | source)
XLA Modules:
  0.0 52.6 jit_solution(13744992785329924200)
XLA Ops:
  0.6 51.2 %phase_linking.1 = (f32[4,2,32,128]{3,2,1,0:T(8,128)S(1)}, f32[2,2,32,128]{3,2,1,0:T(8,128)S(1)}, f32[2,1,32]{2,1,0:T(1,128)S(1)}) custom-call(f32[2,160,640]{2,1,0:T(8,128)} %amp_hbm.1, f32[2,160,640]{2,1,0:T(8,128)} %ph_hbm.1, s32[4,2,128]{2,1,0:T(2,128)} %bitcast.5, s32[4,128]{1,0:T(4,128)} %bitcast.6, s32[1,128]{1,0:T(1,128)} %bitcast.7), custom_call_target="tpu_custom_call" | custom-call | tf_op jit(solution)/shard_map/phase_linking/pallas_call | solution.py:565
  51.9 0.7 %write_out.1 = (f32[4,2,32,128]{3,2,1,0:T(8,128)}, f32[2,2,32,128]{3,2,1,0:T(8,128)}, f32[2,1,32]{2,1,0:T(1,128)}) custom-call(f32[4,2,32,128]{3,2,1,0:T(8,128)S(1)} %get-tuple-element.6.ifg_in, f32[2,2,32,128]{3,2,1,0:T(8,128)S(1)} %get-tuple-element.7.link_in, f32[2,1,32]{2,1,0:T(1,128)S(1)} %get-tuple-element.8.qual_in), custom_call_target="tpu_custom_call" | custom-call | tf_op jit(solution)/shard_map/write_out/pallas_call | solution.py:607

commit v4 on v3

--- a/solution.py
+++ b/solution.py
@@ -14,7 +14,7 @@
 ITERS = 8
 TILE_CAP = 2
 EPS = 1e-06
-BACK = 6
+BACK = 5
 SLOT = 16
 ROWS = 10
 HALO = 8
@@ -444,14 +444,26 @@
                 vr, vi = u_high[2 * b], u_high[2 * b + 1]
                 qual = qual + edge[f, mid, :] * (ur * vr + ui * vi)
                 qual = qual - edge[f + 1, mid, :] * (ur * vi - ui * vr)
-    qual = jnp.sum(qual, axis=0, keepdims=True)
+    nmsg[0:1, :] = kappa
+    nmsg[1:2, :] = jnp.sum(qual, axis=0, keepdims=True)
+
+    for i in range(1, planes):
+        target = wrap(me + i * columns, devices)
+        remote(nmsg, nbuf.at[plane], n_send, n_recv, target).start()
+    nbuf[plane] = nmsg[...]
+    await_bytes(nbuf.at[pl.ds(0, planes - 1)], n_recv)
+    both = nbuf[0]
+    for i in range(1, planes):
+        both = both + nbuf[i]
+    kappa, qual = both[0:1, :], both[1:2, :]
+    alpha = 1.0 / jnp.sqrt(kappa)
+    qual = qual / (kappa * pairs_total)
 
     for g in range(columns // SUB):
         cut = slice(SUB + HALO + SUB * g, SUB + HALO + SUB * (g + 1))
         for f in range(4):
-            umsg[pl.ds(SUB * SUB * g + f, SUB, stride=SUB), :] = vec[last, f, cut, :]
-        umsg[pl.ds(SUB * SUB * g + 4, SUB, stride=SUB), :] = jnp.broadcast_to(kappa, (SUB, LANES))
-        umsg[pl.ds(SUB * SUB * g + 5, SUB, stride=SUB), :] = jnp.broadcast_to(qual, (SUB, LANES))
+            umsg[pl.ds(SUB * SUB * g + f, SUB, stride=SUB), :] = vec[last, f, cut, :] * alpha
+        umsg[pl.ds(SUB * SUB * g + 4, SUB, stride=SUB), :] = jnp.broadcast_to(qual, (SUB, LANES))
 
     def back_rows(slot):
         return pl.ds(pl.multiple_of(SUB * slot, SUB), BACK)
@@ -486,37 +498,15 @@
     def back(f, g):
         return ubuf[pl.ds(SUB * SUB * g + f, SUB, stride=SUB), :]
 
-    def picked(x):
-        return lax.dot_general(
-            pick[...], x, (((1,), (1,)), ((), ())),
-            precision=lax.Precision.HIGHEST, preferred_element_type=F32,
-        )
-
     await_bytes(ubuf.at[pl.ds(0, (columns - 1) * BACK), :], u_recv)
-    for g in range(columns // SUB):
-        nmsg[SUB * g : SUB * (g + 1), :] = back(4, g)
-    quality = jnp.concatenate([back(5, g) for g in range(columns // SUB)], axis=0)
-    nmsg[columns : columns + SUB, 0:columns] = picked(quality)
-    nmsg[columns : columns + SUB, columns:] = jnp.zeros((SUB, LANES - columns), F32)
-    for i in range(1, planes):
-        target = lax.rem(plane + i, planes) * columns + cs
-        remote(nmsg, nbuf.at[plane], n_send, n_recv, target).start()
-    nbuf[plane] = nmsg[...]
-
-    await_bytes(nbuf.at[pl.ds(0, planes - 1)], n_recv)
-    scale = nbuf[0]
-    for i in range(1, planes):
-        scale = scale + nbuf[i]
-    kappa = scale[0:columns]
-    alpha = 1.0 / jnp.sqrt(kappa)
     for g in range(columns // SUB):
         cut = slice(SUB * g, SUB * (g + 1))
         for f in range(4):
-            link_ref[f // 2, f % 2, cut, :] = back(f, g) * alpha[cut]
-    norm = picked(kappa) * pairs_total
-    held = norm > 0.0
-    chosen[...] = jnp.where(
-        held, scale[columns:, 0:columns] / jnp.where(held, norm, 1.0), 0.0
+            link_ref[f // 2, f % 2, cut, :] = back(f, g)
+    quality = jnp.concatenate([back(4, g) for g in range(columns // SUB)], axis=0)
+    chosen[...] = lax.dot_general(
+        pick[...], quality, (((1,), (1,)), ((), ())),
+        precision=lax.Precision.HIGHEST, preferred_element_type=F32,
     )
     for a in range(TILE_CAP):
         qual_ref[a] = chosen[pl.ds(plane * TILE_CAP + a, 1), :]
@@ -593,8 +583,8 @@
             pltpu.VMEM((2, rows_w, LANES), F32),
             pltpu.VMEM((columns * SUB, LANES), F32),
             pltpu.VMEM((columns * SUB, LANES), F32),
-            pltpu.VMEM((columns + SUB, LANES), F32),
-            pltpu.VMEM((planes, columns + SUB, LANES), F32),
+            pltpu.VMEM((2, LANES), F32),
+            pltpu.VMEM((planes, 2, LANES), F32),
             pltpu.VMEM((SUB, LANES), F32),
             pltpu.VMEM((SUB, columns), F32),
             dma((2, 4)), dma((3,)), dma((2, 2)), dma((2, 2)), dma((2, 2)), dma((2, 2)),

time: 52.9 us -> 52.2 us (0.987)
  Pallas kernels: 51.9 us -> 51.2 us
    pallas_call x1, Pallas kernels: 51.2 us -> 50.5 us  [per_device(): pl.pallas_call(kernel, name='phase_linking', out_shape=(jax.ShapeDtypeStr...]
where the time goes in v4:
time: 52.2 us; the launch traced here: 51.9 us
  Pallas kernels  51.2 us (98%)
  between operations  0.64 us (1%)
    pallas_call x1, Pallas kernels, per_device(): pl.pallas_call(kernel, name='phase_linking', out_shape=(jax.ShapeDtypeStr...  50.5 us

profile of v4, /device:TPU:32, one launch (start us, length us, event | category | flops | bytes accessed | tf_op | source)
XLA Modules:
  0.0 51.9 jit_solution(6670345165326396675)
XLA Ops:
  0.6 50.5 %phase_linking.1 = (f32[4,2,32,128]{3,2,1,0:T(8,128)S(1)}, f32[2,2,32,128]{3,2,1,0:T(8,128)S(1)}, f32[2,1,32]{2,1,0:T(1,128)S(1)}) custom-call(f32[2,160,640]{2,1,0:T(8,128)} %amp_hbm.1, f32[2,160,640]{2,1,0:T(8,128)} %ph_hbm.1, s32[4,2,128]{2,1,0:T(2,128)} %bitcast.5, s32[4,128]{1,0:T(4,128)} %bitcast.6, s32[1,128]{1,0:T(1,128)} %bitcast.7), custom_call_target="tpu_custom_call" | custom-call | tf_op jit(solution)/shard_map/phase_linking/pallas_call | solution.py:555
  51.2 0.7 %write_out.1 = (f32[4,2,32,128]{3,2,1,0:T(8,128)}, f32[2,2,32,128]{3,2,1,0:T(8,128)}, f32[2,1,32]{2,1,0:T(1,128)}) custom-call(f32[4,2,32,128]{3,2,1,0:T(8,128)S(1)} %get-tuple-element.6.ifg_in, f32[2,2,32,128]{3,2,1,0:T(8,128)S(1)} %get-tuple-element.7.link_in, f32[2,1,32]{2,1,0:T(1,128)S(1)} %get-tuple-element.8.qual_in), custom_call_target="tpu_custom_call" | custom-call | tf_op jit(solution)/shard_map/write_out/pallas_call | solution.py:597
